TPU v7x, 512 devices: a whole 4x8x8 slice. The times are simulated.
512 devices in a mesh: dp: 16 (over x, y_hi), ep: 32 (over y_lo, z, core).
Axes of the slice: x: 4, y: 8 (y_hi: 4, y_lo: 2; y = y_hi * 2 + y_lo), z: 8, core: 2. Of those that a mesh axis runs over, the one named last changes fastest.
Arguments:
- tokens: bfloat16 [65536, 2048], P(('dp', 'ep')), may hold values from -6 to 6
- cotangent: bfloat16 [65536, 2048], P(('dp', 'ep')), may hold values from -6 to 6
- expert_ids: int32 [65536, 8], P(('dp', 'ep')), may hold values from 0 to 31, all different within a row; in each aligned block of 128 rows (0 to 127, 128 to 255, ...) at most 34 rows name the same one
- gate_weights: bfloat16 [65536, 8], P(('dp', 'ep')), may hold values from 0.019897461 to 0.3984375
- w_up: bfloat16 [32, 2048, 384], P('ep'), may hold values from -0.125 to 0.125
- w_down: bfloat16 [32, 2048, 384], P('ep'), may hold values from -0.3125 to 0.3125
Outputs:
- token_grad: bfloat16 [65536, 2048], P(('dp', 'ep'))
- gate_grad: bfloat16 [65536, 8], P(('dp', 'ep'))
- down_grad: float32 [32, 2048, 384], P('ep', 'dp')
Inputs may be any that keep to these rules, and one draw needn't show every extreme that they name: `expert_ids`: each token names 8 different experts; among the 128 tokens of one device (aligned blocks of rows) no expert is named more than 34 times, and in some block one expert is named exactly 34 times.
All inputs are finite; a program needn't handle non-finite values.
Results may differ from a plain program's by a relative error of at most 0.008.
Values may be sent and summed in bfloat16 or wider, within the bound.
A program may use at most 128 MiB of HBM per device.

v0:
```python
import jax
import jax.numpy as jnp
from jax import lax
from jax.sharding import PartitionSpec as P


def expert_forward(tokens_in, w_up):
    pre_act = jnp.einsum("sbcd,bdh->sbch", tokens_in, w_up, preferred_element_type=jnp.float32)
    hidden = jax.nn.silu(pre_act).astype(jnp.bfloat16)
    return (pre_act, hidden)


def shards(tokens, cotangent, expert_ids, gate_weights, w_up, w_down):
    tok_rows, width = tokens.shape
    top_count = expert_ids.shape[1]
    ep_count = lax.axis_size("ep")
    local_experts = w_up.shape[0]
    experts_total = local_experts * ep_count
    base_load = tok_rows * top_count // experts_total
    capacity = base_load + max(1, base_load // 16)
    route_count = tok_rows * top_count
    flat_ids = expert_ids.reshape(route_count)
    expert_hits = (
        expert_ids[:, :, None] == jnp.arange(experts_total, dtype=jnp.int32)[None, None, :]
    ).astype(jnp.bfloat16)
    token_counts = jnp.sum(expert_hits, axis=1)
    row_index = jnp.arange(tok_rows, dtype=jnp.int32)
    lower_ones = (row_index[:, None] > row_index[None, :]).astype(jnp.bfloat16)
    prior_counts = jnp.dot(lower_ones, token_counts, preferred_element_type=jnp.float32)
    earlier = (
        jnp.sum(expert_hits.astype(jnp.float32) * prior_counts[:, None, :], axis=2)
        .astype(jnp.int32)
        .reshape(route_count)
    )
    buffer_pos = flat_ids * capacity + earlier
    slot_total = experts_total * capacity
    inverse = jnp.full((slot_total,), route_count, jnp.int32)
    inverse = inverse.at[buffer_pos].set(jnp.arange(route_count, dtype=jnp.int32))
    occupied = inverse < route_count
    route_of = jnp.minimum(inverse, route_count - 1)
    token_of = route_of // top_count
    blank = jnp.zeros((), jnp.bfloat16)
    x_send = jnp.where(occupied[:, None], tokens[token_of], blank)
    dy_send = jnp.where(occupied[:, None], cotangent[token_of], blank)
    g_send = jnp.where(occupied, gate_weights.reshape(route_count)[route_of], blank)
    layout = (ep_count, local_experts, capacity, width)
    x_recv, dy_recv, g_recv = (
        lax.all_to_all(x_send, "ep", split_axis=0, concat_axis=0, tiled=True),
        lax.all_to_all(dy_send, "ep", split_axis=0, concat_axis=0, tiled=True),
        lax.all_to_all(g_send, "ep", split_axis=0, concat_axis=0, tiled=True),
    )
    pre_act, hidden = expert_forward(x_recv.reshape(layout), w_up)
    dy_in = dy_recv.reshape(layout)
    gate_f = g_recv.reshape(ep_count, local_experts, capacity).astype(jnp.float32)[..., None]
    back_hidden = jnp.einsum("sbcd,bdh->sbch", dy_in, w_down, preferred_element_type=jnp.float32)
    gate_slots = jnp.sum(back_hidden * hidden.astype(jnp.float32), axis=3).astype(jnp.bfloat16)
    sig = jax.nn.sigmoid(pre_act)
    slope = sig * (1.0 + pre_act * (1.0 - sig))
    grad_pre = (gate_f * back_hidden * slope).astype(jnp.bfloat16)
    route_grad = jnp.einsum(
        "sbch,bdh->sbcd", grad_pre, w_up, preferred_element_type=jnp.float32
    ).astype(jnp.bfloat16)
    scaled_cot = (gate_f * dy_in).astype(jnp.bfloat16)
    back_grad, back_gate = (
        lax.all_to_all(
            route_grad.reshape(slot_total, width), "ep", split_axis=0, concat_axis=0, tiled=True
        ),
        lax.all_to_all(
            gate_slots.reshape(slot_total), "ep", split_axis=0, concat_axis=0, tiled=True
        ),
    )
    token_grad = jnp.sum(
        back_grad[buffer_pos].reshape(tok_rows, top_count, width), axis=1, dtype=jnp.float32
    ).astype(jnp.bfloat16)
    gate_grad = back_gate[buffer_pos].reshape(tok_rows, top_count)
    partial_grad = jnp.einsum(
        "sbcd,sbch->bdh", scaled_cot, hidden, preferred_element_type=jnp.float32
    )
    down_grad = lax.psum_scatter(partial_grad, "dp", scatter_dimension=1, tiled=True)
    return (token_grad, gate_grad, down_grad)


def solution(mesh):
    return jax.shard_map(
        shards,
        mesh=mesh,
        in_specs=(
            P(("dp", "ep"), None),
            P(("dp", "ep"), None),
            P(("dp", "ep"), None),
            P(("dp", "ep"), None),
            P("ep", None, None),
            P("ep", None, None),
        ),
        out_specs=(P(("dp", "ep"), None), P(("dp", "ep"), None), P("ep", "dp", None)),
        check_vma=False,
    )
```

profile of v0, /device:TPU:1, one launch (start us, length us, event | category | flops | bytes accessed | tf_op | source)
XLA Modules:
  0.0 515.0 jit_solution(16706136737465446325)
XLA Ops:
  7.2 0.8 fusion.23
  8.0 0.1 fusion.24
  8.1 0.7 multiply_reduce_fusion
  8.9 0.7 convert_add_fusion
  9.6 0.8 copy.29
  10.7 4.3 scatter_custom_fusion
  15.1 6.9 %gather_fusion = bf16[1088]{0:T(1024)(128)(2,1)S(1)} fusion(bf16[1024]{0:T(1024)(128)(2,1)S(1)} %reshape.144, s32[2048]{0:T(1024)S(1)} %get-tuple-element.24), kind=kCustom, calls=%fused_computation | custom fusion | bytes 8704 | tf_op jit(solution)/shard_map/gather | solution.py:45
  22.0 0.7 all_to_all.34
  22.7 13.0 %all-to-all-start = ((bf16[32,34,1]{1,2,0:T(2,128)(2,1)}), bf16[32,34,1]{1,2,0:T(2,128)(2,1)S(1)}, u32[]{:S(2)}, u32[]{:S(2)}) async-start(bf16[32,34,1]{1,2,0:T(2,128)(2,1)} %all_to_all.34), calls=%async_computation | async-start | bytes 32768 | tf_op jit(solution)/shard_map/all_to_all | solution.py:50
  35.7 0.1 broadcast_in_dim.42
  35.9 5.9 %gather_fusion.2 = bf16[1088,2048]{1,0:T(8,128)(2,1)} fusion(bf16[128,2048]{1,0:T(8,128)(2,1)S(1)} %copy-done.1, s32[2048]{0:T(1024)S(1)} %get-tuple-element.23), kind=kCustom, calls=%fused_computation.2 | custom fusion | bytes 8917248 | tf_op jit(solution)/shard_map/gather | solution.py:43
  41.7 7.3 %gather.23 = bf16[32,34,2048]{2,1,0:T(8,128)(2,1)} reshape(bf16[1088,2048]{1,0:T(8,128)(2,1)} %gather_fusion.2) | data formatting | bytes 8912896 | tf_op jit(solution)/shard_map/gather | solution.py:43
  49.1 5.9 %gather_fusion.1 = bf16[1088,2048]{1,0:T(8,128)(2,1)} fusion(bf16[128,2048]{1,0:T(8,128)(2,1)S(1)} %copy-done.2, s32[2048]{0:T(1024)S(1)} %get-tuple-element.23), kind=kCustom, calls=%fused_computation.1 | custom fusion | bytes 8917248 | tf_op jit(solution)/shard_map/gather | solution.py:44
  55.0 7.3 %gather.21 = bf16[32,34,2048]{2,1,0:T(8,128)(2,1)} reshape(bf16[1088,2048]{1,0:T(8,128)(2,1)} %gather_fusion.1) | data formatting | bytes 8912896 | tf_op jit(solution)/shard_map/gather | solution.py:44
  62.3 8.8 %broadcast_select_fusion = (bf16[32,34,2048]{2,1,0:T(8,128)(2,1)}, bf16[32,34,2048]{2,1,0:T(8,128)(2,1)}) fusion(bf16[32,34,2048]{2,1,0:T(8,128)(2,1)} %gather.23, pred[32,34]{1,0:T(8,128)(4,1)S(1)} %broadcast_in_dim.42, bf16[32,34,2048]{2,1,0:T(8,128)(2,1)} %gather.21), kind=kLoop, calls=%fused_computation.9 | loop fusion | flops 4456448 | bytes 17826880 | tf_op jit(solution)/shard_map/jit(_where)/select_n | solution.py:43
  71.1 125.5 %all_to_all.40 = bf16[32,34,2048]{2,1,0:T(8,128)(2,1)} all-to-all(bf16[32,34,2048]{2,1,0:T(8,128)(2,1)} %get-tuple-element.19), channel_id=1, replica_groups=mesh['dp'=16,'ep'=32] {'ep'}, dimensions={0} | all-to-all | bytes 8912896 | tf_op jit(solution)/shard_map/all_to_all | solution.py:48
  196.6 5.7 %all-to-all-start.1 = ((bf16[32,34,2048]{2,1,0:T(8,128)(2,1)}), bf16[32,34,2048]{2,1,0:T(8,128)(2,1)}, u32[]{:S(2)}, u32[]{:S(2)}) async-start(bf16[32,34,2048]{2,1,0:T(8,128)(2,1)} %get-tuple-element.20), calls=%async_computation.1 | async-start | bytes 10485760 | tf_op jit(solution)/shard_map/all_to_all | solution.py:49
  202.4 6.7 %fusion.13 = f32[32,34,384]{2,1,0:T(8,128)} fusion(bf16[32,34,2048]{2,1,0:T(8,128)(2,1)} %all_to_all.40, bf16[1,2048,384]{2,1,0:T(8,128)(2,1)S(1)} %copy-done), kind=kOutput, calls=%fused_computation.29 | convolution fusion | flops 1711276032 | bytes 7700480 | tf_op jit(solution)/shard_map/sbcd,bdh->sbch/dot_general | solution.py:8
  209.0 117.8 %all-to-all-done.1 = bf16[32,34,2048]{2,1,0:T(8,128)(2,1)} async-done(((bf16[32,34,2048]{2,1,0:T(8,128)(2,1)}), bf16[32,34,2048]{2,1,0:T(8,128)(2,1)}, u32[]{:S(2)}, u32[]{:S(2)}) %all-to-all-start.1) | async-done | bytes 4456480 | tf_op jit(solution)/shard_map/all_to_all | solution.py:49
  326.8 7.9 %fusion.5 = (bf16[32,34]{1,0:T(8,128)(2,1)S(1)}, f32[32,34,384]{2,1,0:T(8,128)}) fusion(f32[32,34,384]{2,1,0:T(8,128)} %fusion.13, bf16[32,34,2048]{2,1,0:T(8,128)(2,1)} %all-to-all-done.1, bf16[1,2048,384]{2,1,0:T(8,128)(2,1)} %param.11), kind=kOutput, calls=%fused_computation.18 | convolution fusion | flops 1714617344 | bytes 9373824 | tf_op jit(solution)/shard_map/sbcd,bdh->sbch/dot_general | solution.py:55
  334.7 0.6 copy.31
  335.3 9.6 %all-to-all-start.4 = ((bf16[32,34,1]{1,2,0:T(2,128)(2,1)}), bf16[32,34,1]{1,2,0:T(2,128)(2,1)S(1)}, u32[]{:S(2)}, u32[]{:S(2)}) async-start(bf16[32,34,1]{1,2,0:T(2,128)(2,1)} %copy.31), calls=%async_computation.4 | async-start | bytes 32768 | tf_op jit(solution)/shard_map/all_to_all | solution.py:68
  344.9 7.7 %convolution_convert_fusion = bf16[32,34,2048]{2,1,0:T(8,128)(2,1)} fusion(bf16[1,2048,384]{2,1,0:T(8,128)(2,1)S(1)} %copy-done, f32[32,34,384]{2,1,0:T(8,128)} %get-tuple-element.22, f32[32,34,384]{2,1,0:T(8,128)} %fusion.13, f32[32,34]{1,0:T(8,128)S(1)} %bitcast.82), kind=kOutput, calls=%fused_computation.12 | convolution fusion | flops 1717682176 | bytes 9376000 | tf_op jit(solution)/shard_map/sbch,bdh->sbcd/dot_general | solution.py:60
  352.7 8.3 %all-to-all-start.3 = ((bf16[32,34,2048]{2,1,0:T(8,128)(2,1)}), bf16[32,34,2048]{2,1,0:T(8,128)(2,1)}, u32[]{:S(2)}, u32[]{:S(2)}) async-start(bf16[32,34,2048]{2,1,0:T(8,128)(2,1)} %convolution_convert_fusion), calls=%async_computation.3 | async-start | bytes 10485760 | tf_op jit(solution)/shard_map/all_to_all | solution.py:65
  361.1 7.8 %fusion.2 = f32[1,2048,384]{2,1,0:T(8,128)} fusion(bf16[32,34,2048]{2,1,0:T(8,128)(2,1)} %all-to-all-done.1, f32[32,34]{1,0:T(8,128)S(1)} %bitcast.83, f32[32,34,384]{2,1,0:T(8,128)} %fusion.13), kind=kOutput, calls=%fused_computation.13 | convolution fusion | flops 1720049664 | bytes 9277696 | tf_op jit(solution)/shard_map/sbcd,sbch->bdh/dot_general | solution.py:76
  369.0 0.1 all_to_all.33
  369.1 6.8 %gather_fusion.4 = bf16[1024]{0:T(1024)(128)(2,1)S(1)} fusion(bf16[1088]{0:T(1024)(128)(2,1)S(1)} %all_to_all.33, s32[1024]{0:T(1024)S(1)} %broadcast_clamp_fusion), kind=kCustom, calls=%fused_computation.4 | custom fusion | bytes 8192 | tf_op jit(solution)/shard_map/gather | solution.py:75
  376.0 0.7 copy.32
  376.7 106.6 %all-to-all-done.3 = bf16[32,34,2048]{2,1,0:T(8,128)(2,1)} async-done(((bf16[32,34,2048]{2,1,0:T(8,128)(2,1)}), bf16[32,34,2048]{2,1,0:T(8,128)(2,1)}, u32[]{:S(2)}, u32[]{:S(2)}) %all-to-all-start.3) | async-done | bytes 4456480 | tf_op jit(solution)/shard_map/all_to_all | solution.py:65
  483.3 7.3 %all_to_all.31 = bf16[1088,2048]{1,0:T(8,128)(2,1)} reshape(bf16[32,34,2048]{2,1,0:T(8,128)(2,1)} %all-to-all-done.3) | data formatting | bytes 8912896 | tf_op jit(solution)/shard_map/all_to_all | solution.py:65
  490.6 11.7 %gather_fusion.3 = bf16[1024,2048]{1,0:T(8,128)(2,1)} fusion(bf16[1088,2048]{1,0:T(8,128)(2,1)} %all_to_all.31, s32[1024]{0:T(1024)S(1)} %broadcast_clamp_fusion), kind=kCustom, calls=%fused_computation.3 | custom fusion | bytes 8392704 | tf_op jit(solution)/shard_map/gather | solution.py:73
  502.3 5.9 %bitcast_reduce_fusion = bf16[128,2048]{1,0:T(8,128)(2,1)} fusion(bf16[1024,2048]{1,0:T(8,128)(2,1)} %gather_fusion.3), kind=kLoop, calls=%fused_computation.11 | loop fusion | flops 1835008 | bytes 4718592 | tf_op jit(solution)/shard_map/reduce_sum | solution.py:72
  (23 shorter events, 0.7 us)
Async XLA Ops:
  7.2 195.2 %copy-start = (bf16[1,2048,384]{2,1,0:T(8,128)(2,1)S(1)}, bf16[1,2048,384]{2,1,0:T(8,128)(2,1)}, u32[]{:S(2)}) copy-start(bf16[1,2048,384]{2,1,0:T(8,128)(2,1)} %param.10) | copy-start | bytes 4718596
  15.1 20.8 %copy-start.1 = (bf16[128,2048]{1,0:T(8,128)(2,1)S(1)}, bf16[128,2048]{1,0:T(8,128)(2,1)}, u32[]{:S(2)}) copy-start(bf16[128,2048]{1,0:T(8,128)(2,1)} %param.6) | copy-start | bytes 1572868
  22.7 48.4 %all-to-all-start = ((bf16[32,34,1]{1,2,0:T(2,128)(2,1)}), bf16[32,34,1]{1,2,0:T(2,128)(2,1)S(1)}, u32[]{:S(2)}, u32[]{:S(2)}) async-start(bf16[32,34,1]{1,2,0:T(2,128)(2,1)} %all_to_all.34), calls=%async_computation | async-start | bytes 32768 | tf_op jit(solution)/shard_map/all_to_all | solution.py:50
  41.7 7.4 %copy-start.2 = (bf16[128,2048]{1,0:T(8,128)(2,1)S(1)}, bf16[128,2048]{1,0:T(8,128)(2,1)}, u32[]{:S(2)}) copy-start(bf16[128,2048]{1,0:T(8,128)(2,1)} %param.7) | copy-start | bytes 1572868
  196.6 130.2 %all-to-all-start.1 = ((bf16[32,34,2048]{2,1,0:T(8,128)(2,1)}), bf16[32,34,2048]{2,1,0:T(8,128)(2,1)}, u32[]{:S(2)}, u32[]{:S(2)}) async-start(bf16[32,34,2048]{2,1,0:T(8,128)(2,1)} %get-tuple-element.20), calls=%async_computation.1 | async-start | bytes 10485760 | tf_op jit(solution)/shard_map/all_to_all | solution.py:49
  335.3 17.4 %all-to-all-start.4 = ((bf16[32,34,1]{1,2,0:T(2,128)(2,1)}), bf16[32,34,1]{1,2,0:T(2,128)(2,1)S(1)}, u32[]{:S(2)}, u32[]{:S(2)}) async-start(bf16[32,34,1]{1,2,0:T(2,128)(2,1)} %copy.31), calls=%async_computation.4 | async-start | bytes 32768 | tf_op jit(solution)/shard_map/all_to_all | solution.py:68
  352.7 130.6 %all-to-all-start.3 = ((bf16[32,34,2048]{2,1,0:T(8,128)(2,1)}), bf16[32,34,2048]{2,1,0:T(8,128)(2,1)}, u32[]{:S(2)}, u32[]{:S(2)}) async-start(bf16[32,34,2048]{2,1,0:T(8,128)(2,1)} %convolution_convert_fusion), calls=%async_computation.3 | async-start | bytes 10485760 | tf_op jit(solution)/shard_map/all_to_all | solution.py:65
  361.0 147.2 %reduce-scatter.2.cloned.1.call-start = ((), (), s32[]{:S(2)}) async-start(), calls=%async_computation.6 | async-start | bytes 3342336 | tf_op jit(solution)/shard_map/reduce_scatter | solution.py:79
Sparse Core Ops, SparseCore 0:
  369.0 101.0 reduce-scatter.1
where the time goes:
time: 517 us; the launch traced here: 515 us
  waiting for transfers between devices  224 us (43%)
  blocking collectives  126 us (24%)
  local copies, waits for them, and re-layouts  66.9 us (13%)
  starting transfers between devices  36.6 us (7%)
  matrix products  30.2 us (6%)
  other arithmetic  17.1 us (3%)
  between operations  14.2 us (3%)
    all_to_all x1, blocking collectives, shards(): lax.all_to_all(x_send, 'ep', split_axis=0, concat_axis=0, tiled=True)  126 us
    all_to_all x1, waiting for transfers between devices, shards(): lax.all_to_all(dy_send, 'ep', split_axis=0, concat_axis=0, tiled=True)  118 us
    all_to_all x1, waiting for transfers between devices, shards(): lax.all_to_all(route_grad.reshape(slot_total, width), 'ep', split_axis=0,...  107 us
    gather x2, local copies, waits for them, and re-layouts, shards(): x_send = jnp.where(occupied[:, None], tokens[token_of], blank)  13.2 us
    gather x2, local copies, waits for them, and re-layouts, shards(): dy_send = jnp.where(occupied[:, None], cotangent[token_of], blank)  13.2 us
    all_to_all x1, starting transfers between devices, shards(): lax.all_to_all(g_send, 'ep', split_axis=0, concat_axis=0, tiled=True)  13 us
    gather x1, local copies, waits for them, and re-layouts, shards(): back_grad[buffer_pos].reshape(tok_rows, top_count, width)  11.7 us
  transfers between devices with their start and end apart: 5, of which 3 were waited for; matrix products, arithmetic and copies ran while one was open for 16% of the time, Pallas kernels for 0%

commit v1 on v0

v1 whole, which is shorter than its diff:
```python
import jax
import jax.numpy as jnp
from jax import lax
from jax.experimental import pallas as pl
from jax.experimental.pallas import tpu as pltpu
from jax.sharding import PartitionSpec as P

MESH = pl.DeviceIdType.MESH
BF16, F32 = jnp.bfloat16, jnp.float32
NX, NYH, NZ = 4, 4, 8
NY = 2 * NYH
ROWS = 128
LANES = 128
HALF = 1024


def kernel(
    xg_ref, dy_ref, wu_ref, wd_ref, tok_ref, gg_ref, dg_ref,
    xb, db, wu, wd, gh, gp, pre_s, bh_s, pb, rb, dyt, a_s, s_s, r_s, x1, x2, yr,
    loc_sem, ag_send, ag_recv, w_send, w_recv, rs_send, rs_recv, c_send, c_recv, x_send, x_recv, y_send, y_recv,
):
    width = dy_ref.shape[1]
    hid_n = wu_ref.shape[2]
    wide = xg_ref.shape[1]
    dp, ep = lax.axis_index("dp"), lax.axis_index("ep")
    core = lax.rem(ep, 2)
    z = lax.rem(ep // 2, NZ)
    yl = ep // (2 * NZ)
    x, yh = dp // NYH, lax.rem(dp, NYH)
    yy = 2 * yh + yl

    def dev(x_, y_, z_, c_):
        return (x_ * NYH + y_ // 2, (lax.rem(y_, 2) * NZ + z_) * 2 + c_)

    zdev = [dev(x, yy, lax.rem(z + 1, NZ), core), dev(x, yy, lax.rem(z + NZ - 1, NZ), core)]
    cdev = dev(x, yy, z, 1 - core)
    ydev = [None] + [dev(x, lax.rem(yy + d, NY), z, core) for d in range(1, NY)]
    y_pair = dev(x, lax.rem(yy + NY + 1 - 2 * yl, NY), z, core)
    y_other = dev(x, lax.rem(yy + NY + 2 * yl - 1, NY), z, core)
    xdev = [dev(lax.rem(x + 1, NX), yy, z, core), dev(lax.rem(x + NX - 1, NX), yy, z, core)]

    barrier = pltpu.get_barrier_semaphore()
    partners = zdev + [cdev] + ydev[1:] + xdev
    for device in partners:
        pl.semaphore_signal(barrier, inc=1, device_id=device, device_id_type=MESH)

    own = [
        pltpu.make_async_copy(xg_ref, xb.at[pl.ds(0, ROWS)], loc_sem.at[0]),
        pltpu.make_async_copy(dy_ref, db.at[pl.ds(0, ROWS)], loc_sem.at[1]),
        pltpu.make_async_copy(wu_ref.at[0], wu.at[0], loc_sem.at[2]),
        pltpu.make_async_copy(wd_ref.at[0], wd.at[0], loc_sem.at[3]),
    ]
    for copy in own:
        copy.start()
    pl.semaphore_wait(barrier, len(partners))

    def remote(src, dst, ssem, rsem, device):
        return pltpu.make_async_remote_copy(
            src_ref=src, dst_ref=dst, send_sem=ssem, recv_sem=rsem,
            device_id=device, device_id_type=MESH,
        )

    bufs = (xb, db)

    def block(arr, start):
        return bufs[arr].at[pl.ds(pl.multiple_of(start, ROWS), ROWS)]

    for arr, src in enumerate((xg_ref, dy_ref)):
        for r in range(2):
            remote(
                src, block(arr, (2 + r) * ROWS), ag_send.at[arr, r, 0], ag_recv.at[arr, r, 1], zdev[r]
            ).start()
    part = width // 2
    weight_first = []
    for m, (src, buf, far) in enumerate(((wu_ref, wu, y_pair), (wd_ref, wd, y_other))):
        for h in range(2):
            rows = pl.ds(h * part, part)
            weight_first.append(remote(
                src.at[0, rows], buf.at[2, rows], w_send.at[m, h, 0], w_recv.at[m, h, 0], far))
    for copy in weight_first:
        copy.start()
    weight_core = []
    for m, (src, buf) in enumerate(((wu_ref, wu), (wd_ref, wd))):
        for h in range(2):
            rows = pl.ds(h * part, part)
            weight_core.append(remote(
                src.at[0, rows], buf.at[1, rows], w_send.at[m, h, 1], w_recv.at[m, h, 1], cdev))
    for copy in weight_core:
        copy.start()
    weight_relay = []
    for m, buf in enumerate((wu, wd)):
        for h in range(2):
            rows = pl.ds(h * part, part)
            weight_relay.append(remote(
                buf.at[2, rows], buf.at[3, rows], w_send.at[m, h, 2], w_recv.at[m, h, 2], cdev))

    def ring_row(s, r):
        return jnp.where(s == 4, ROWS, (2 * s + r) * ROWS)

    lane = lax.broadcasted_iota(jnp.int32, (1, LANES), 1)
    chunk = 32

    def ring_step(i, carry):
        s = i + 1
        for arr in range(2):
            for r in range(2):
                def arrive(arr=arr, r=r):
                    here = block(arr, ring_row(s, r))
                    remote(here, here, ag_send.at[arr, r, 0], ag_recv.at[arr, r, s], zdev[r]).wait_recv()

                    @pl.when(s <= (3 if arr == r else 2))
                    def _():
                        remote(
                            here, block(arr, ring_row(s + 1, r)),
                            ag_send.at[arr, r, s], ag_recv.at[arr, r, s + 1], zdev[r],
                        ).start()

                if arr == r:
                    arrive()
                else:
                    pl.when(s <= 3)(arrive)

        @pl.when(i == 0)
        def _():
            for h in range(2):
                for m in range(2):
                    weight_first[2 * m + h].wait_recv()
                    weight_relay[2 * m + h].start()
            for copy in weight_core:
                copy.wait_recv()
            for copy in own:
                copy.wait()
            for copy in weight_relay:
                copy.wait_recv()

        base = pl.multiple_of(jnp.where(i == 3, 0, (i + 1) * 2 * ROWS), 2 * ROWS)
        rows = pl.ds(base, 2 * ROWS)
        pb[rows, width:] = jnp.zeros((2 * ROWS, LANES), BF16)

        def expert(j, carry):
            yl_j = jnp.where(j < 2, yl, 1 - yl)
            c_j = jnp.where(lax.rem(j, 2) == 0, core, 1 - core)
            e = (yl_j * NZ + z) * 2 + c_j
            pre_s[...] = jnp.dot(xb[rows, :width], wu[j], preferred_element_type=F32)
            bh_s[...] = jnp.dot(db[rows, :], wd[j], preferred_element_type=F32)

            def piece(q, carry):
                at = pl.multiple_of(q * chunk, chunk)
                sub = pl.ds(at, chunk)
                big = pl.ds(pl.multiple_of(base + at, chunk), chunk)
                mine = lane == e
                g = jnp.sum(jnp.where(mine, xb[big, width:].astype(F32), 0.0), axis=1, keepdims=True)
                pre, bh = pre_s[sub, :], bh_s[sub, :]
                sig = 0.5 * jnp.tanh(0.5 * pre) + 0.5
                hidden = (pre * sig).astype(BF16).astype(F32)
                gate = jnp.sum(bh * hidden, axis=1, keepdims=True)
                slope = sig * (1.0 + pre * (1.0 - sig))
                gp[j, sub, :] = (g * bh * slope).astype(BF16)
                gh[j, big, :] = (g * hidden).astype(BF16)
                pb[big, width:] = jnp.where(mine, gate, pb[big, width:].astype(F32)).astype(BF16)
                return carry

            return lax.fori_loop(0, 2 * ROWS // chunk, piece, carry)

        lax.fori_loop(0, 4, expert, 0)

        def columns(t, carry):
            at = pl.ds(pl.multiple_of(t * 512, 512), 512)
            total = None
            for j in range(4):
                term = lax.dot_general(
                    gp[j], wu[j, at, :], (((1,), (1,)), ((), ())), preferred_element_type=F32)
                total = term if total is None else total + term
            pb[rows, at] = total.astype(BF16)
            return carry

        lax.fori_loop(0, width // 512, columns, 0)
        return carry

    lax.fori_loop(0, 4, ring_step, 0)

    cols = (pl.ds(0, HALF), pl.ds(HALF, wide - HALF))
    back = (zdev[1], zdev[0])

    def rs_copy(r, t, h):
        row = ROWS if t == 0 else (2 * (4 - t) + r) * ROWS
        return remote(
            pb.at[pl.ds(row, ROWS), cols[h]], rb.at[r, t, :, cols[h]],
            rs_send.at[r, t, h], rs_recv.at[r, t, h], back[r])

    for r in range(2):
        rs_copy(r, 0, r).start()
    for r in range(2):
        rs_copy(r, 1, 1 - r).start()

    def rs_step(t):
        order = [(r, h) for h in ((0, 1)) for r in range(2)]
        order = [(r, r ^ k) for k in ((1, 0)) for r in range(2)] if t > 1 else [(r, r) for r in range(2)]
        for r, h in order:
            rs_copy(r, t - 1, h).wait_recv()
            row = pl.ds((2 * (4 - t) + r) * ROWS, ROWS)
            pb[row, cols[h]] = (
                pb[row, cols[h]].astype(F32) + rb[r, t - 1, :, cols[h]].astype(F32)).astype(BF16)
            rs_copy(r, t, h).start()

    tile = width // NX

    def down_tile(q, carry):
        d = jnp.where(q == 0, 2, jnp.where(q == 3, 0, jnp.where(q == 2, 3, 1)))
        at = pl.ds(pl.multiple_of(lax.rem(x + d, NX) * tile, tile), tile)

        def flip(k, carry):
            sub = pl.ds(pl.multiple_of(k * ROWS, ROWS), ROWS)
            dyt[:, sub] = db[sub, at].T
            return carry

        lax.fori_loop(0, NZ, flip, 0)

        def pair(jj, carry):
            s_s[q, jj] = jnp.dot(dyt[...], gh[2 * jj + 1], preferred_element_type=F32).astype(BF16)
            a_s[q, jj] = jnp.dot(dyt[...], gh[2 * jj], preferred_element_type=F32).astype(BF16)
            return carry

        lax.fori_loop(0, 2, pair, 0)
        remote(s_s.at[q], r_s.at[q], c_send.at[q], c_recv.at[q], cdev).start()
        return carry

    lax.fori_loop(0, NX, down_tile, 0)
    rs_step(1)

    def core_copy(q):
        return remote(s_s.at[q], r_s.at[q], c_send.at[q], c_recv.at[q], cdev)

    def add_into(dst, *others):
        total = dst[...].astype(F32)
        for other in others:
            total = total + other[...].astype(F32)
        dst[...] = total.astype(BF16)

    def x_first(r):
        return remote(a_s.at[0, r], x1.at[r], x_send.at[0, r], x_recv.at[0, r], xdev[r])

    def x_second(r):
        return remote(a_s.at[1 + r], x2.at[r], x_send.at[1, r], x_recv.at[1, r], xdev[r])

    core_copy(0).wait_recv()
    for jj in range(2):
        add_into(a_s.at[0, jj], r_s.at[0, jj])
    for r in range(2):
        x_first(r).start()
    for q in (1, 2, 3):
        core_copy(q).wait_recv()
        for jj in range(2):
            add_into(a_s.at[q, jj], r_s.at[q, jj])
    rs_step(2)
    for r in range(2):
        x_first(r).wait_recv()
        add_into(a_s.at[1 + r, r], x1.at[r])
        x_second(r).start()
    rs_step(3)
    for r in range(2):
        x_second(r).wait_recv()
    for jj in range(2):
        add_into(a_s.at[3, jj], x2.at[0, jj], x2.at[1, jj])

    def y_copy(d):
        row = pl.multiple_of((lax.rem(yy + d, NY) // 2) * ROWS, ROWS)
        return remote(
            a_s.at[3, d % 2, pl.ds(row, ROWS)], yr.at[d - 1], y_send.at[d - 1], y_recv.at[d - 1], ydev[d])

    for d in range(1, NY):
        y_copy(d).start()

    for r in range(2):
        for h in range(2):
            rs_copy(r, 3, h).wait_recv()
    first = pl.ds(0, ROWS)
    final = pb[first, :].astype(F32) + rb[0, 3].astype(F32) + rb[1, 3].astype(F32)
    tok_ref[...] = final[:, :width].astype(BF16)
    gg_ref[...] = final[:, width:].astype(BF16)

    total = a_s[3, 0, pl.ds(pl.multiple_of(yh * ROWS, ROWS), ROWS), :].astype(F32)
    for d in range(1, NY):
        y_copy(d).wait_recv()
        total = total + yr[d - 1].astype(F32)
    dg_ref[...] = total

    for arr in range(2):
        for r in range(2):
            for s in range(4 if arr == r else 3):
                here = block(arr, 0)
                remote(here, here, ag_send.at[arr, r, s], ag_recv.at[arr, r, 1], zdev[r]).wait_send()
    for copy in weight_first + weight_core + weight_relay:
        copy.wait_send()
    for r in range(2):
        rs_copy(r, 0, r).wait_send()
        for t in range(1, 4):
            for h in range(2):
                rs_copy(r, t, h).wait_send()
        x_first(r).wait_send()
        x_second(r).wait_send()
    for q in range(NX):
        core_copy(q).wait_send()
    for d in range(1, NY):
        y_copy(d).wait_send()


def shards(tokens, cotangent, expert_ids, gate_weights, w_up, w_down):
    rows, width = tokens.shape
    hid_n = w_up.shape[2]
    wide = width + LANES
    experts = jnp.arange(LANES, dtype=jnp.int32)
    hits = expert_ids[:, :, None] == experts[None, None, :]
    dense = jnp.sum(jnp.where(hits, gate_weights.astype(F32)[:, :, None], 0.0), axis=1).astype(BF16)
    xg = jnp.concatenate([tokens, dense], axis=1)
    tile = width // NX
    dma, vmem = pltpu.SemaphoreType.DMA, pltpu.VMEM
    hbm = pl.BlockSpec(memory_space=pl.ANY)
    token_grad, gates, down = pl.pallas_call(
        kernel,
        out_shape=(
            jax.ShapeDtypeStruct((rows, width), BF16),
            jax.ShapeDtypeStruct((rows, LANES), BF16),
            jax.ShapeDtypeStruct((width // (NX * NYH), hid_n), F32),
        ),
        in_specs=[hbm] * 4,
        out_specs=[pl.BlockSpec(memory_space=pltpu.VMEM)] * 3,
        scratch_shapes=[
            vmem((NZ * rows, wide), BF16),
            vmem((NZ * rows, width), BF16),
            vmem((4, width, hid_n), BF16),
            vmem((4, width, hid_n), BF16),
            vmem((4, NZ * rows, hid_n), BF16),
            vmem((4, 2 * rows, hid_n), BF16),
            vmem((2 * rows, hid_n), F32),
            vmem((2 * rows, hid_n), F32),
            vmem((NZ * rows, wide), BF16),
            vmem((2, 4, rows, wide), BF16),
            vmem((tile, NZ * rows), BF16),
            vmem((NX, 2, tile, hid_n), BF16),
            vmem((NX, 2, tile, hid_n), BF16),
            vmem((NX, 2, tile, hid_n), BF16),
            vmem((2, tile, hid_n), BF16),
            vmem((2, 2, tile, hid_n), BF16),
            vmem((NY - 1, rows, hid_n), BF16),
            dma((4,)),
            dma((2, 2, 4)),
            dma((2, 2, 5)),
            dma((2, 2, 3)),
            dma((2, 2, 3)),
            dma((2, 4, 2)),
            dma((2, 4, 2)),
            dma((NX,)),
            dma((NX,)),
            dma((2, 2)),
            dma((2, 2)),
            dma((NY - 1,)),
            dma((NY - 1,)),
        ],
        compiler_params=pltpu.CompilerParams(
            collective_id=0, has_side_effects=True, vmem_limit_bytes=66_000_000
        ),
        name="expert_backward",
    )(xg, cotangent, w_up, w_down)
    picked = jnp.where(hits, gates.astype(F32)[:, None, :], 0.0)
    gate_grad = jnp.sum(picked, axis=2).astype(BF16)
    return token_grad, gate_grad, down[None]


def solution(mesh):
    return jax.shard_map(
        shards,
        mesh=mesh,
        in_specs=(
            P(("dp", "ep"), None),
            P(("dp", "ep"), None),
            P(("dp", "ep"), None),
            P(("dp", "ep"), None),
            P("ep", None, None),
            P("ep", None, None),
        ),
        out_specs=(P(("dp", "ep"), None), P(("dp", "ep"), None), P("ep", "dp", None)),
        check_vma=False,
    )
```

time: 517 us -> 187 us (0.36)
  waiting for transfers between devices: 224 us -> 0 us
  Pallas kernels: 0 us -> 178 us
  blocking collectives: 126 us -> 0 us
  local copies, waits for them, and re-layouts: 66.9 us -> 4.79 us
  starting transfers between devices: 36.6 us -> 0 us
  matrix products: 30.2 us -> 0 us
  other arithmetic: 17.1 us -> 3.43 us
  between operations: 14.2 us -> 0.65 us
    all_to_all x4 -> x0, waiting for transfers between devices: 224 us -> none  [the longest x1 118 us: shards(): lax.all_to_all(dy_send, 'ep', split_axis=0, concat_axis=0, tiled=True)]
    pallas_call x0 -> x1, Pallas kernels: none -> 178 us  [shards(): pl.pallas_call(kernel, out_shape=(jax.ShapeDtypeStruct((rows, width), BF1...]
    all_to_all x1 -> x0, blocking collectives: 126 us -> none  [shards(): lax.all_to_all(x_send, 'ep', split_axis=0, concat_axis=0, tiled=True)]
    gather x7 -> x0, local copies, waits for them, and re-layouts: 51.8 us -> none  [the longest x2 13.2 us: shards(): x_send = jnp.where(occupied[:, None], tokens[token_of], blank)]
    all_to_all x4 -> x0, starting transfers between devices: 36.6 us -> none  [the longest x1 13 us: shards(): lax.all_to_all(g_send, 'ep', split_axis=0, concat_axis=0, tiled=True)]
    dot_general x5 -> x0, matrix products: 30.2 us -> none  [the longest x1 7.88 us: shards(): jnp.einsum('sbcd,bdh->sbch', dy_in, w_down, preferred_element_type=jnp.fl...]
    select_n x4 -> x0, other arithmetic: 8.85 us -> none  [the longest x1 8.82 us: shards(): x_send = jnp.where(occupied[:, None], tokens[token_of], blank)]
    all_to_all x3 -> x0, local copies, waits for them, and re-layouts: 8.17 us -> none  [the longest x1 7.34 us: shards(): lax.all_to_all(route_grad.reshape(slot_total, width), 'ep', split_axis=0,...]
  transfers between devices with their start and end apart: 5 -> 0, of which waited for: 3 -> 0; matrix products, arithmetic and copies ran while one was open for 16% -> 0% of each run, Pallas kernels for 0% -> 0%
where the time goes in v1:
time: 187 us
  Pallas kernels  178 us (95%)
  local copies, waits for them, and re-layouts  4.79 us (3%)
  other arithmetic  3.43 us (2%)
    pallas_call x1, Pallas kernels, shards(): pl.pallas_call(kernel, out_shape=(jax.ShapeDtypeStruct((rows, width), BF1...  178 us
    unnamed x6, local copies, waits for them, and re-layouts  4.01 us

profile of v1, /device:TPU:1, one launch (start us, length us, event | category | flops | bytes accessed | tf_op | source)
XLA Modules:
  0.0 187.0 jit_solution(3333042982656091733)
XLA Ops:
  0.6 0.8 copy.11
  1.4 0.8 copy.12
  2.2 0.4 select_reduce_fusion.1
  2.6 1.9 %pad_maximum_fusion.xg_ref = bf16[128,2176]{1,0:T(8,128)(2,1)} fusion(bf16[128,128]{1,0:T(8,128)(2,1)S(1)} %select_reduce_fusion.1, bf16[128,2048]{1,0:T(8,128)(2,1)} %param.6), kind=kLoop, calls=%fused_computation | loop fusion | flops 1114112 | bytes 1114112 | tf_op jit(solution)/shard_map/concatenate | solution.py:315
  4.4 178.1 %expert_backward.1 = (bf16[128,2048]{1,0:T(8,128)(2,1)}, bf16[128,128]{1,0:T(8,128)(2,1)}, f32[128,384]{1,0:T(8,128)}) custom-call(bf16[128,2176]{1,0:T(8,128)(2,1)} %pad_maximum_fusion.xg_ref, bf16[128,2048]{1,0:T(8,128)(2,1)} %dy_ref.1, bf16[1,2048,384]{2,1,0:T(8,128)(2,1)} %wu_ref.1, bf16[1,2048,384]{2,1,0:T(8,128)(2,1)} %wd_ref.1), custom_call_target="tpu_custom_call" | custom-call | tf_op jit(solution)/shard_map/expert_backward/pallas_call | solution.py:319
  182.6 0.0 copy-start
  182.6 0.8 convert_element_type.14
  183.4 0.4 select_reduce_fusion
  183.8 0.7 copy.13
  184.4 1.9 %copy.16 = bf16[128,2048]{1,0:T(8,128)(2,1)} copy(bf16[128,2048]{1,0:T(8,128)(2,1)} %get-tuple-element.15) | data formatting | bytes 1048576
  186.3 0.0 copy-done
  186.3 0.7 copy.17
Async XLA Ops:
  182.6 3.7 %copy-start = (f32[128,384]{1,0:T(8,128)S(1)}, f32[128,384]{1,0:T(8,128)}, u32[]{:S(2)}) copy-start(f32[128,384]{1,0:T(8,128)} %get-tuple-element.8) | copy-start | bytes 589828

commit v2 on v0

v2 whole, which is shorter than its diff:
```python
import jax
import jax.numpy as jnp
from jax import lax
from jax.experimental import pallas as pl
from jax.experimental.pallas import tpu as pltpu
from jax.sharding import PartitionSpec as P

MESH = pl.DeviceIdType.MESH
BF16, F32 = jnp.bfloat16, jnp.float32
NX, NYH, NZ = 4, 4, 8
NY = 2 * NYH
ROWS = 128
LANES = 128
HALF = 1024
EXP = 32


def kernel(
    x_ref, dy_ref, wu_ref, wd_ref, ids_ref, gates_ref, tok_ref, gg_ref, dg_ref,
    xb, db, gt, wu, wd, gh, gp, pre_s, bh_s, gs, gq, pb, pg, rb, rg, dyt, a_s, s_s, r_s, x1, x2, yr,
    loc_sem, ag_send, ag_recv, w_send, w_recv, rs_send, rs_recv, c_send, c_recv, x_send, x_recv, y_send, y_recv,
):
    width = dy_ref.shape[1]
    hid_n = wu_ref.shape[2]
    tile = width // NX
    dp, ep = lax.axis_index("dp"), lax.axis_index("ep")
    core = lax.rem(ep, 2)
    z = lax.rem(ep // 2, NZ)
    yl = ep // (2 * NZ)
    x, yh = dp // NYH, lax.rem(dp, NYH)
    yy = 2 * yh + yl

    def dev(x_, y_, z_, c_):
        return (x_ * NYH + y_ // 2, (lax.rem(y_, 2) * NZ + z_) * 2 + c_)

    zdev = [dev(x, yy, lax.rem(z + 1, NZ), core), dev(x, yy, lax.rem(z + NZ - 1, NZ), core)]
    cdev = dev(x, yy, z, 1 - core)
    ydev = [None] + [dev(x, lax.rem(yy + d, NY), z, core) for d in range(1, NY)]
    y_pair = dev(x, lax.rem(yy + NY + 1 - 2 * yl, NY), z, core)
    y_other = dev(x, lax.rem(yy + NY + 2 * yl - 1, NY), z, core)
    xdev = [dev(lax.rem(x + 1, NX), yy, z, core), dev(lax.rem(x + NX - 1, NX), yy, z, core)]

    barrier = pltpu.get_barrier_semaphore()
    partners = zdev + [cdev] + ydev[1:] + xdev
    for device in partners:
        pl.semaphore_signal(barrier, inc=1, device_id=device, device_id_type=MESH)

    OWN, FAR = (NZ - 2) * ROWS, (NZ - 1) * ROWS
    own = [
        pltpu.make_async_copy(x_ref, xb.at[pl.ds(OWN, ROWS)], loc_sem.at[0]),
        pltpu.make_async_copy(dy_ref, db.at[pl.ds(OWN, ROWS)], loc_sem.at[1]),
        pltpu.make_async_copy(wu_ref.at[0], wu.at[:, pl.ds(0, hid_n)], loc_sem.at[2]),
        pltpu.make_async_copy(wd_ref.at[0], wd.at[:, pl.ds(0, hid_n)], loc_sem.at[3]),
    ]
    for copy in own:
        copy.start()
    names = lax.broadcasted_iota(jnp.int32, (EXP, ROWS), 0)
    dense = jnp.zeros((EXP, ROWS), F32)
    for k in range(ids_ref.shape[0]):
        dense = dense + jnp.where(ids_ref[k : k + 1, :] == names, gates_ref[k : k + 1, :].astype(F32), 0.0)
    gt[NZ - 2] = dense.astype(BF16)
    pl.semaphore_wait(barrier, len(partners))

    def remote(src, dst, ssem, rsem, device):
        return pltpu.make_async_remote_copy(
            src_ref=src, dst_ref=dst, send_sem=ssem, recv_sem=rsem,
            device_id=device, device_id_type=MESH,
        )

    bufs = (xb, db)
    last_way = (0, 1, 0)

    def block(arr, k):
        if arr == 2:
            return gt.at[k]
        return bufs[arr].at[pl.ds(k * ROWS, ROWS)]

    def slot(s, r):
        return NZ - 1 if s == 4 else 2 * (s - 1) + r

    sent = []

    def send_block(arr, r, s, src):
        copy = remote(src, block(arr, slot(s, r)), ag_send.at[arr, r, s - 1], ag_recv.at[arr, r, s], zdev[r])
        copy.start()
        sent.append(copy)

    def arrive(arr, s):
        for r in range(2):
            if s == 4 and last_way[arr] != r:
                continue
            here = block(arr, slot(s, r))
            remote(here, here, ag_send.at[arr, r, 0], ag_recv.at[arr, r, s], zdev[r]).wait_recv()
            if s < 3 or (s == 3 and last_way[arr] == r):
                send_block(arr, r, s + 1, here)

    for arr, src in ((0, x_ref), (1, dy_ref), (2, gt.at[NZ - 2])):
        for r in range(2):
            send_block(arr, r, 1, src)
    part = width // 2
    weight_first, weight_core, weight_relay = [], [], []
    for h in range(2):
        for m, (src, buf, far) in enumerate(((wu_ref, wu, y_pair), (wd_ref, wd, y_other))):
            rows = pl.ds(h * part, part)
            lanes = [pl.ds(j * hid_n, hid_n) for j in range(4)]
            weight_first.append(remote(
                src.at[0, rows], buf.at[rows, lanes[1]], w_send.at[m, h, 0], w_recv.at[m, h, 0], far))
            weight_core.append(remote(
                src.at[0, rows], buf.at[rows, lanes[2]], w_send.at[m, h, 1], w_recv.at[m, h, 1], cdev))
            weight_relay.append(remote(
                buf.at[rows, lanes[1]], buf.at[rows, lanes[3]], w_send.at[m, h, 2], w_recv.at[m, h, 2], cdev))
    for copy in weight_first + weight_core:
        copy.start()

    lane = lax.broadcasted_iota(jnp.int32, (1, LANES), 1)
    lane32 = lax.broadcasted_iota(jnp.int32, (1, EXP), 1)
    chunk = 32
    slots = [((yl if j % 2 == 0 else 1 - yl) * NZ + z) * 2 + (core if j < 2 else 1 - core) for j in range(4)]

    def compute(k, blocks):
        base, size = k * ROWS, blocks * ROWS
        rows = pl.ds(base, size)
        for b in range(blocks):
            gs[pl.ds(b * ROWS, ROWS), :] = gt[k + b].astype(F32).T

        def hidden_part(n, carry):
            at = pl.ds(pl.multiple_of(n * 512, 512), 512)
            pre_s[:size, at] = jnp.dot(xb[rows, :], wu[:, at], preferred_element_type=F32)
            bh_s[:size, at] = jnp.dot(db[rows, :], wd[:, at], preferred_element_type=F32)
            return carry

        lax.fori_loop(0, 4 * hid_n // 512, hidden_part, 0)

        def piece(q, carry):
            at = pl.multiple_of(q * chunk, chunk)
            sub = pl.ds(at, chunk)
            big = pl.ds(pl.multiple_of(base + at, chunk), chunk)
            out = jnp.zeros((chunk, LANES), F32)
            for j in range(4):
                lanes = pl.ds(j * hid_n, hid_n)
                g = jnp.sum(jnp.where(lane32 == slots[j], gs[sub, :], 0.0), axis=1, keepdims=True)
                pre, bh = pre_s[sub, lanes], bh_s[sub, lanes]
                sig = 0.5 * jnp.tanh(0.5 * pre) + 0.5
                hidden = (pre * sig).astype(BF16).astype(F32)
                gate = jnp.sum(bh * hidden, axis=1, keepdims=True)
                slope = sig * (1.0 + pre * (1.0 - sig))
                gp[sub, lanes] = (g * bh * slope).astype(BF16)
                gh[big, lanes] = (g * hidden).astype(BF16)
                out = jnp.where(lane == slots[j], gate, out)
            gq[sub, :] = out
            return carry

        lax.fori_loop(0, size // chunk, piece, 0)
        for b in range(blocks):
            pg[k + b] = gq[pl.ds(b * ROWS, ROWS), :].T[:EXP, :].astype(BF16)

        def columns(t, carry):
            at = pl.ds(pl.multiple_of(t * 512, 512), 512)
            pb[rows, at] = lax.dot_general(
                gp[:size, :], wu[at, :], (((1,), (1,)), ((), ())), preferred_element_type=F32).astype(BF16)
            return carry

        lax.fori_loop(0, width // 512, columns, 0)

    deep = NZ * ROWS // 2

    def down_tile(phase):
        def body(q, carry):
            d = jnp.where(q == 0, 2, jnp.where(q == 3, 0, jnp.where(q == 2, 3, 1)))
            at = pl.ds(pl.multiple_of(lax.rem(x + d, NX) * tile, tile), tile)
            for k in range(deep // ROWS):
                dyt[:, pl.ds(k * ROWS, ROWS)] = db[pl.ds(phase * deep + k * ROWS, ROWS), at].T
            rows = pl.ds(phase * deep, deep)
            for dst, start in ((s_s, 2 * hid_n), (a_s, 0)):
                term = jnp.dot(dyt[...], gh[rows, pl.ds(start, 2 * hid_n)], preferred_element_type=F32)
                if phase:
                    term = term + dst[q].astype(F32)
                dst[q] = term.astype(BF16)
            if phase:
                remote(s_s.at[q], r_s.at[q], c_send.at[q], c_recv.at[q], cdev).start()
            return carry
        return body

    cols = (pl.ds(0, HALF), pl.ds(HALF, width - HALF))
    back = (zdev[1], zdev[0])

    def rs_copy(r, t, h):
        k = slot(4 - t, r)
        if h == 2:
            src, dst = pg.at[k], rg.at[r, t]
        else:
            src, dst = pb.at[pl.ds(k * ROWS, ROWS), cols[h]], rb.at[r, t, :, cols[h]]
        return remote(src, dst, rs_send.at[r, t, h], rs_recv.at[r, t, h], back[r])

    def rs_add(r, t, h):
        rs_copy(r, t - 1, h).wait_recv()
        k = slot(4 - t, r)
        if h == 2:
            pg[k] = (pg[k].astype(F32) + rg[r, t - 1].astype(F32)).astype(BF16)
        else:
            row = pl.ds(k * ROWS, ROWS)
            pb[row, cols[h]] = (
                pb[row, cols[h]].astype(F32) + rb[r, t - 1, :, cols[h]].astype(F32)).astype(BF16)
        rs_copy(r, t, h).start()

    def rs_free(t):
        for r in range(2):
            rs_add(r, t, 1 - r)

    def rs_tied(t):
        for r in range(2):
            rs_add(r, t, r)
        for r in range(2):
            if t > 1 or r == 0:
                rs_add(r, t, 2)

    for arr in (0, 1, 2):
        arrive(arr, 1)
    for first, relay in zip(weight_first, weight_relay):
        first.wait_recv()
        relay.start()
    for copy in own:
        copy.wait()
    for copy in weight_core + weight_relay:
        copy.wait_recv()
    compute(NZ - 2, 1)
    arrive(0, 2)
    compute(0, 2)
    arrive(1, 2)
    arrive(2, 2)
    compute(2, 2)
    arrive(0, 3)
    lax.fori_loop(0, NX, down_tile(0), 0)
    arrive(1, 3)
    arrive(2, 3)
    compute(4, 2)
    for r in range(2):
        rs_copy(r, 1, 1 - r).start()
    rs_copy(1, 1, 2).start()
    for arr in (0, 1, 2):
        arrive(arr, 4)
    compute(NZ - 1, 1)
    for r in range(2):
        rs_copy(r, 0, r).start()
    rs_copy(0, 0, 2).start()
    rs_free(2)
    lax.fori_loop(0, 2, down_tile(1), 0)
    rs_tied(1)
    lax.fori_loop(2, NX, down_tile(1), 0)
    rs_free(3)

    def core_copy(q):
        return remote(s_s.at[q], r_s.at[q], c_send.at[q], c_recv.at[q], cdev)

    def add_into(dst, *others):
        total = dst[...].astype(F32)
        for other in others:
            total = total + other[...].astype(F32)
        dst[...] = total.astype(BF16)

    def half(jj):
        return pl.ds(jj * hid_n, hid_n)

    def x_first(r):
        return remote(a_s.at[0, :, half(r)], x1.at[r], x_send.at[0, r, 0], x_recv.at[0, r, 0], xdev[r])

    def x_second(r, jj):
        return remote(
            a_s.at[1 + r, :, half(jj)], x2.at[r, jj], x_send.at[1, r, jj], x_recv.at[1, r, jj], xdev[r])

    core_copy(0).wait_recv()
    add_into(a_s.at[0], r_s.at[0])
    for r in range(2):
        x_first(r).start()
    for r in range(2):
        core_copy(1 + r).wait_recv()
        add_into(a_s.at[1 + r], r_s.at[1 + r])
        x_second(r, 1 - r).start()
    core_copy(3).wait_recv()
    add_into(a_s.at[3], r_s.at[3])
    rs_tied(2)
    for r in range(2):
        x_first(r).wait_recv()
        add_into(a_s.at[1 + r, :, half(r)], x1.at[r])
        x_second(r, r).start()
    rs_tied(3)

    def y_copy(d):
        row = pl.multiple_of((lax.rem(yy + d, NY) // 2) * ROWS, ROWS)
        return remote(
            a_s.at[3, pl.ds(row, ROWS), half(d % 2)], yr.at[d - 1], y_send.at[d - 1], y_recv.at[d - 1], ydev[d])

    for r in range(2):
        x_second(r, 1 - r).wait_recv()
    for r in range(2):
        x_second(r, r).wait_recv()
    for jj in range(2):
        add_into(a_s.at[3, :, half(jj)], x2.at[0, jj], x2.at[1, jj])
        for d in ((4, 2, 6) if jj == 0 else (3, 5, 1, 7)):
            y_copy(d).start()

    mine = pl.ds(OWN, ROWS)
    for h in (1, 0):
        for r in range(2):
            rs_copy(r, 3, r ^ h).wait_recv()
    for h in range(2):
        tok_ref[:, cols[h]] = (
            pb[mine, cols[h]].astype(F32) + rb[0, 3, :, cols[h]].astype(F32) + rb[1, 3, :, cols[h]].astype(F32)
        ).astype(BF16)
    for r in range(2):
        rs_copy(r, 3, 2).wait_recv()
    gates = pg[NZ - 2].astype(F32) + rg[0, 3].astype(F32) + rg[1, 3].astype(F32)
    for k in range(ids_ref.shape[0]):
        picked = jnp.where(ids_ref[k : k + 1, :] == names, gates, 0.0)
        gg_ref[k : k + 1, :] = jnp.sum(picked, axis=0, keepdims=True)

    total = a_s[3, pl.ds(pl.multiple_of(yh * ROWS, ROWS), ROWS), half(0)].astype(F32)
    for d in range(1, NY):
        y_copy(d).wait_recv()
        total = total + yr[d - 1].astype(F32)
    dg_ref[...] = total

    for copy in sent + weight_first + weight_core + weight_relay:
        copy.wait_send()
    for r in range(2):
        for t in range(4):
            for h in range(3):
                if t == 0 and h != (r if h < 2 else 2 + r):
                    continue
                rs_copy(r, t, h).wait_send()
        x_first(r).wait_send()
        for jj in range(2):
            x_second(r, jj).wait_send()
    for q in range(NX):
        core_copy(q).wait_send()
    for d in range(1, NY):
        y_copy(d).wait_send()


def shards(tokens, cotangent, expert_ids, gate_weights, w_up, w_down):
    rows, width = tokens.shape
    hid_n = w_up.shape[2]
    tile = width // NX
    dma, vmem = pltpu.SemaphoreType.DMA, pltpu.VMEM
    hbm = pl.BlockSpec(memory_space=pl.ANY)
    local = pl.BlockSpec(memory_space=pltpu.VMEM)
    token_grad, gates, down = pl.pallas_call(
        kernel,
        out_shape=(
            jax.ShapeDtypeStruct((rows, width), BF16),
            jax.ShapeDtypeStruct((expert_ids.shape[1], rows), F32),
            jax.ShapeDtypeStruct((width // (NX * NYH), hid_n), F32),
        ),
        in_specs=[hbm] * 4 + [local] * 2,
        out_specs=[local] * 3,
        scratch_shapes=[
            vmem((NZ * rows, width), BF16),
            vmem((NZ * rows, width), BF16),
            vmem((NZ, EXP, rows), BF16),
            vmem((width, 4 * hid_n), BF16),
            vmem((width, 4 * hid_n), BF16),
            vmem((NZ * rows, 4 * hid_n), BF16),
            vmem((2 * rows, 4 * hid_n), BF16),
            vmem((2 * rows, 4 * hid_n), F32),
            vmem((2 * rows, 4 * hid_n), F32),
            vmem((2 * rows, EXP), F32),
            vmem((2 * rows, LANES), F32),
            vmem((NZ * rows, width), BF16),
            vmem((NZ, EXP, rows), BF16),
            vmem((2, 4, rows, width), BF16),
            vmem((2, 4, EXP, rows), BF16),
            vmem((tile, NZ * rows // 2), BF16),
            vmem((NX, tile, 2 * hid_n), BF16),
            vmem((NX, tile, 2 * hid_n), BF16),
            vmem((NX, tile, 2 * hid_n), BF16),
            vmem((2, tile, hid_n), BF16),
            vmem((2, 2, tile, hid_n), BF16),
            vmem((NY - 1, rows, hid_n), BF16),
            dma((4,)),
            dma((3, 2, 4)),
            dma((3, 2, 5)),
            dma((2, 2, 3)),
            dma((2, 2, 3)),
            dma((2, 4, 3)),
            dma((2, 4, 3)),
            dma((NX,)),
            dma((NX,)),
            dma((2, 2, 2)),
            dma((2, 2, 2)),
            dma((NY - 1,)),
            dma((NY - 1,)),
        ],
        compiler_params=pltpu.CompilerParams(
            collective_id=0, has_side_effects=True, vmem_limit_bytes=66_000_000
        ),
        name="expert_backward",
    )(tokens, cotangent, w_up, w_down, expert_ids.T, gate_weights.T)
    return token_grad, gates.T.astype(BF16), down[None]


def solution(mesh):
    return jax.shard_map(
        shards,
        mesh=mesh,
        in_specs=(
            P(("dp", "ep"), None),
            P(("dp", "ep"), None),
            P(("dp", "ep"), None),
            P(("dp", "ep"), None),
            P("ep", None, None),
            P("ep", None, None),
        ),
        out_specs=(P(("dp", "ep"), None), P(("dp", "ep"), None), P("ep", "dp", None)),
        check_vma=False,
    )
```

time: 517 us -> 162 us (0.31)
  the two profiles are of different devices: /device:TPU:1 before, /device:TPU:64 now
where the time goes in v2:
time: 162 us
  Pallas kernels  156 us (96%)
  local copies, waits for them, and re-layouts  3.5 us (2%)
    pallas_call x1, Pallas kernels, shards(): pl.pallas_call(kernel, out_shape=(jax.ShapeDtypeStruct((rows, width), BF1...  156 us
    unnamed x2, local copies, waits for them, and re-layouts  3.5 us

profile of v2, /device:TPU:64, one launch (start us, length us, event | category | flops | bytes accessed | tf_op | source)
XLA Modules:
  0.0 161.6 jit_solution(15700405582986764059)
XLA Ops:
  0.6 156.2 %expert_backward.1 = (bf16[128,2048]{1,0:T(8,128)(2,1)}, f32[8,128]{1,0:T(8,128)}, f32[128,384]{1,0:T(8,128)}) custom-call(bf16[128,2048]{1,0:T(8,128)(2,1)} %x_ref.1, bf16[128,2048]{1,0:T(8,128)(2,1)} %dy_ref.1, bf16[1,2048,384]{2,1,0:T(8,128)(2,1)} %wu_ref.1, bf16[1,2048,384]{2,1,0:T(8,128)(2,1)} %wd_ref.1, s32[8,128]{1,0:T(8,128)} %bitcast.6, ...), custom_call_target="tpu_custom_call" | custom-call | tf_op jit(solution)/shard_map/expert_backward/pallas_call | solution.py:347
  156.9 1.3 convert_bitcast_fusion
  158.1 1.9 %copy.11 = bf16[128,2048]{1,0:T(8,128)(2,1)} copy(bf16[128,2048]{1,0:T(8,128)(2,1)} %get-tuple-element.12) | data formatting | bytes 1048576
  160.0 1.6 copy.12

commit v3 on v2

--- a/solution.py
+++ b/solution.py
@@ -13,12 +13,13 @@
 LANES = 128
 HALF = 1024
 EXP = 32
+MID = 64
 
 
 def kernel(
     x_ref, dy_ref, wu_ref, wd_ref, ids_ref, gates_ref, tok_ref, gg_ref, dg_ref,
-    xb, db, gt, wu, wd, gh, gp, pre_s, bh_s, gs, gq, pb, pg, rb, rg, dyt, a_s, s_s, r_s, x1, x2, yr,
-    loc_sem, ag_send, ag_recv, w_send, w_recv, rs_send, rs_recv, c_send, c_recv, x_send, x_recv, y_send, y_recv,
+    xb, db, gt, wu, wd, gh, gp, pre_s, bh_s, gs, gq, pb, pg, rb, rg, dyt, a1, a2, s1, s2, r1, r2, rx1, ry1, ry2, rx2,
+    loc_sem, ag_send, ag_recv, w_send, w_recv, rs_send, rs_recv, c_send, c_recv, x_sems, y1_sems, y2_sems, x2_sems,
 ):
     width = dy_ref.shape[1]
     hid_n = wu_ref.shape[2]
@@ -35,13 +36,13 @@
 
     zdev = [dev(x, yy, lax.rem(z + 1, NZ), core), dev(x, yy, lax.rem(z + NZ - 1, NZ), core)]
     cdev = dev(x, yy, z, 1 - core)
-    ydev = [None] + [dev(x, lax.rem(yy + d, NY), z, core) for d in range(1, NY)]
+    ydev = [dev(x, lax.rem(yy + 1, NY), z, core), dev(x, lax.rem(yy + NY - 1, NY), z, core)]
     y_pair = dev(x, lax.rem(yy + NY + 1 - 2 * yl, NY), z, core)
     y_other = dev(x, lax.rem(yy + NY + 2 * yl - 1, NY), z, core)
     xdev = [dev(lax.rem(x + 1, NX), yy, z, core), dev(lax.rem(x + NX - 1, NX), yy, z, core)]
 
     barrier = pltpu.get_barrier_semaphore()
-    partners = zdev + [cdev] + ydev[1:] + xdev
+    partners = zdev + [cdev] + ydev + xdev
     for device in partners:
         pl.semaphore_signal(barrier, inc=1, device_id=device, device_id_type=MESH)
 
@@ -162,6 +163,10 @@
 
         lax.fori_loop(0, width // 512, columns, 0)
 
+    def core_copy(q, part):
+        src, dst = ((s1.at[q], r1.at[q]), (s2.at[:, q], r2.at[:, q]))[part]
+        return remote(src, dst, c_send.at[q, part], c_recv.at[q, part], cdev)
+
     deep = NZ * ROWS // 2
 
     def down_tile(phase):
@@ -171,13 +176,22 @@
             for k in range(deep // ROWS):
                 dyt[:, pl.ds(k * ROWS, ROWS)] = db[pl.ds(phase * deep + k * ROWS, ROWS), at].T
             rows = pl.ds(phase * deep, deep)
-            for dst, start in ((s_s, 2 * hid_n), (a_s, 0)):
+            for by_x, by_y, start in ((s1, s2, 2 * hid_n), (a1, a2, 0)):
                 term = jnp.dot(dyt[...], gh[rows, pl.ds(start, 2 * hid_n)], preferred_element_type=F32)
-                if phase:
-                    term = term + dst[q].astype(F32)
-                dst[q] = term.astype(BF16)
+                for jj in range(2):
+                    for row in range(NYH):
+                        top = row * ROWS
+                        upper = term[top : top + MID, jj * hid_n : (jj + 1) * hid_n]
+                        lower = term[top + MID : top + ROWS, jj * hid_n : (jj + 1) * hid_n]
+                        k = lax.rem(2 * row + (yl if jj == 0 else 1 - yl) + NY - yy, NY)
+                        if phase:
+                            upper = upper + by_x[q, jj, row].astype(F32)
+                            lower = lower + by_y[k, q].astype(F32)
+                        by_x[q, jj, row] = upper.astype(BF16)
+                        by_y[k, q] = lower.astype(BF16)
             if phase:
-                remote(s_s.at[q], r_s.at[q], c_send.at[q], c_recv.at[q], cdev).start()
+                for half in range(2):
+                    core_copy(q, half).start()
             return carry
         return body
 
@@ -249,55 +263,102 @@
     lax.fori_loop(2, NX, down_tile(1), 0)
     rs_free(3)
 
-    def core_copy(q):
-        return remote(s_s.at[q], r_s.at[q], c_send.at[q], c_recv.at[q], cdev)
-
     def add_into(dst, *others):
         total = dst[...].astype(F32)
         for other in others:
             total = total + other[...].astype(F32)
         dst[...] = total.astype(BF16)
 
-    def half(jj):
-        return pl.ds(jj * hid_n, hid_n)
-
-    def x_first(r):
-        return remote(a_s.at[0, :, half(r)], x1.at[r], x_send.at[0, r, 0], x_recv.at[0, r, 0], xdev[r])
-
-    def x_second(r, jj):
-        return remote(
-            a_s.at[1 + r, :, half(jj)], x2.at[r, jj], x_send.at[1, r, jj], x_recv.at[1, r, jj], xdev[r])
-
-    core_copy(0).wait_recv()
-    add_into(a_s.at[0], r_s.at[0])
-    for r in range(2):
-        x_first(r).start()
-    for r in range(2):
-        core_copy(1 + r).wait_recv()
-        add_into(a_s.at[1 + r], r_s.at[1 + r])
-        x_second(r, 1 - r).start()
-    core_copy(3).wait_recv()
-    add_into(a_s.at[3], r_s.at[3])
+    class Ring:
+        def __init__(self, n, piece, recv, sems, devices):
+            self.n, self.piece, self.recv, self.sems, self.devices = n, piece, recv, sems, devices
+            self.started = []
+
+        def copy(self, r, t, h):
+            m = self.n // 2 - t
+            return remote(
+                self.piece(m if r == 0 else self.n - m, h), self.recv.at[r, t, h],
+                self.sems.at[0, r, t, h], self.sems.at[1, r, t, h], self.devices[r])
+
+        def send(self, r, t, h):
+            self.copy(r, t, h).start()
+            self.started.append((r, t, h))
+
+        def begin(self):
+            for r in range(2):
+                self.send(r, 0, r)
+
+        def forward(self, t, free):
+            for r in range(2):
+                h = 1 - r if free else r
+                if t > 1 or not free:
+                    m = self.n // 2 - t
+                    self.copy(r, t - 1, h).wait_recv()
+                    add_into(self.piece(m if r == 0 else self.n - m, h), self.recv.at[r, t - 1, h])
+                self.send(r, t, h)
+
+        def finish(self):
+            t = self.n // 2 - 1
+            for free in (1, 0):
+                for r in range(2):
+                    self.copy(r, t, 1 - r if free else r).wait_recv()
+            for h in range(2):
+                add_into(self.piece(0, h), self.recv.at[0, t, h], self.recv.at[1, t, h])
+
+        def drain(self):
+            for r, t, h in self.started:
+                self.copy(r, t, h).wait_send()
+
+    place = {2: 0, 1: 1, NX - 1: 2, 0: 3}
+    sub = MID // 2
+
+    def y_row(k):
+        return lax.rem(yy + k, NY) // 2
+
+    ring_x1 = Ring(NX, lambda k, h: a1.at[place[k], h], rx1, x_sems, xdev)
+    ring_y1 = Ring(NY, lambda k, h: a1.at[3, k % 2, y_row(k), pl.ds(h * sub, sub)], ry1, y1_sems, ydev)
+    ring_y2 = Ring(NY, lambda k, h: a2.at[k, pl.ds(2 * h, 2)], ry2, y2_sems, ydev)
+    ring_x2 = Ring(NX, lambda k, h: a2.at[0, place[k], pl.ds(h * sub, sub)], rx2, x2_sems, xdev)
+
+    for q in range(3):
+        core_copy(q, 0).wait_recv()
+        for jj in range(2):
+            add_into(a1.at[q, jj], r1.at[q, jj])
+        if q == 0:
+            ring_x1.begin()
+    ring_x1.forward(1, True)
+    for q in range(NX):
+        core_copy(q, 1).wait_recv()
+    for k in (NY // 2, 3, 5):
+        add_into(a2.at[k], r2.at[k])
+        if k == NY // 2:
+            ring_y2.begin()
+    ring_y2.forward(1, True)
+    for k in (2, 6, 1, 7, 0):
+        add_into(a2.at[k], r2.at[k])
+    core_copy(3, 0).wait_recv()
+    for jj in range(2):
+        add_into(a1.at[3, jj], r1.at[3, jj])
+    ring_x1.forward(1, False)
+    ring_y2.forward(2, True)
+    ring_y2.forward(1, False)
     rs_tied(2)
-    for r in range(2):
-        x_first(r).wait_recv()
-        add_into(a_s.at[1 + r, :, half(r)], x1.at[r])
-        x_second(r, r).start()
+    ring_y2.forward(3, True)
+    ring_y2.forward(2, False)
+    ring_x1.finish()
+    ring_y1.begin()
+    ring_y1.forward(1, True)
+    ring_y2.forward(3, False)
     rs_tied(3)
-
-    def y_copy(d):
-        row = pl.multiple_of((lax.rem(yy + d, NY) // 2) * ROWS, ROWS)
-        return remote(
-            a_s.at[3, pl.ds(row, ROWS), half(d % 2)], yr.at[d - 1], y_send.at[d - 1], y_recv.at[d - 1], ydev[d])
-
-    for r in range(2):
-        x_second(r, 1 - r).wait_recv()
-    for r in range(2):
-        x_second(r, r).wait_recv()
-    for jj in range(2):
-        add_into(a_s.at[3, :, half(jj)], x2.at[0, jj], x2.at[1, jj])
-        for d in ((4, 2, 6) if jj == 0 else (3, 5, 1, 7)):
-            y_copy(d).start()
+    ring_y1.forward(2, True)
+    ring_y1.forward(1, False)
+    ring_y2.finish()
+    ring_x2.begin()
+    ring_x2.forward(1, True)
+    ring_y1.forward(3, True)
+    ring_y1.forward(2, False)
+    ring_x2.forward(1, False)
+    ring_y1.forward(3, False)
 
     mine = pl.ds(OWN, ROWS)
     for h in (1, 0):
@@ -314,11 +375,10 @@
         picked = jnp.where(ids_ref[k : k + 1, :] == names, gates, 0.0)
         gg_ref[k : k + 1, :] = jnp.sum(picked, axis=0, keepdims=True)
 
-    total = a_s[3, pl.ds(pl.multiple_of(yh * ROWS, ROWS), ROWS), half(0)].astype(F32)
-    for d in range(1, NY):
-        y_copy(d).wait_recv()
-        total = total + yr[d - 1].astype(F32)
-    dg_ref[...] = total
+    ring_x2.finish()
+    dg_ref[MID:, :] = a2[0, 3].astype(F32)
+    ring_y1.finish()
+    dg_ref[:MID, :] = a1[3, 0, yh].astype(F32)
 
     for copy in sent + weight_first + weight_core + weight_relay:
         copy.wait_send()
@@ -328,13 +388,11 @@
                 if t == 0 and h != (r if h < 2 else 2 + r):
                     continue
                 rs_copy(r, t, h).wait_send()
-        x_first(r).wait_send()
-        for jj in range(2):
-            x_second(r, jj).wait_send()
     for q in range(NX):
-        core_copy(q).wait_send()
-    for d in range(1, NY):
-        y_copy(d).wait_send()
+        for half in range(2):
+            core_copy(q, half).wait_send()
+    for ring in (ring_x1, ring_y1, ring_y2, ring_x2):
+        ring.drain()
 
 
 def shards(tokens, cotangent, expert_ids, gate_weights, w_up, w_down):
@@ -370,12 +428,16 @@
             vmem((2, 4, rows, width), BF16),
             vmem((2, 4, EXP, rows), BF16),
             vmem((tile, NZ * rows // 2), BF16),
-            vmem((NX, tile, 2 * hid_n), BF16),
-            vmem((NX, tile, 2 * hid_n), BF16),
-            vmem((NX, tile, 2 * hid_n), BF16),
-            vmem((2, tile, hid_n), BF16),
-            vmem((2, 2, tile, hid_n), BF16),
-            vmem((NY - 1, rows, hid_n), BF16),
+            vmem((NX, 2, NYH, MID, hid_n), BF16),
+            vmem((NY, NX, MID, hid_n), BF16),
+            vmem((NX, 2, NYH, MID, hid_n), BF16),
+            vmem((NY, NX, MID, hid_n), BF16),
+            vmem((NX, 2, NYH, MID, hid_n), BF16),
+            vmem((NY, NX, MID, hid_n), BF16),
+            vmem((2, 2, 2, NYH, MID, hid_n), BF16),
+            vmem((2, 4, 2, MID // 2, hid_n), BF16),
+            vmem((2, 4, 2, 2, MID, hid_n), BF16),
+            vmem((2, 2, 2, MID // 2, hid_n), BF16),
             dma((4,)),
             dma((3, 2, 4)),
             dma((3, 2, 5)),
@@ -383,12 +445,12 @@
             dma((2, 2, 3)),
             dma((2, 4, 3)),
             dma((2, 4, 3)),
-            dma((NX,)),
-            dma((NX,)),
-            dma((2, 2, 2)),
-            dma((2, 2, 2)),
-            dma((NY - 1,)),
-            dma((NY - 1,)),
+            dma((NX, 2)),
+            dma((NX, 2)),
+            dma((2, 2, 2, 2)),
+            dma((2, 2, 4, 2)),
+            dma((2, 2, 4, 2)),
+            dma((2, 2, 2, 2)),
         ],
         compiler_params=pltpu.CompilerParams(
             collective_id=0, has_side_effects=True, vmem_limit_bytes=66_000_000

time: 162 us -> 156 us (0.963)
  the two profiles are of different devices: /device:TPU:64 before, /device:TPU:4 now
where the time goes in v3:
time: 156 us
  Pallas kernels  150 us (96%)
  local copies, waits for them, and re-layouts  3.5 us (2%)
    pallas_call x1, Pallas kernels, shards(): pl.pallas_call(kernel, out_shape=(jax.ShapeDtypeStruct((rows, width), BF1...  150 us
    unnamed x2, local copies, waits for them, and re-layouts  3.5 us

profile of v3, /device:TPU:4, one launch (start us, length us, event | category | flops | bytes accessed | tf_op | source)
XLA Modules:
  0.0 155.9 jit_solution(11977879745965016807)
XLA Ops:
  0.6 150.5 %expert_backward.1 = (bf16[128,2048]{1,0:T(8,128)(2,1)}, f32[8,128]{1,0:T(8,128)}, f32[128,384]{1,0:T(8,128)}) custom-call(bf16[128,2048]{1,0:T(8,128)(2,1)} %x_ref.1, bf16[128,2048]{1,0:T(8,128)(2,1)} %dy_ref.1, bf16[1,2048,384]{2,1,0:T(8,128)(2,1)} %wu_ref.1, bf16[1,2048,384]{2,1,0:T(8,128)(2,1)} %wd_ref.1, s32[8,128]{1,0:T(8,128)} %bitcast.6, ...), custom_call_target="tpu_custom_call" | custom-call | tf_op jit(solution)/shard_map/expert_backward/pallas_call | solution.py:405
  151.1 1.3 convert_bitcast_fusion
  152.4 1.9 %copy.11 = bf16[128,2048]{1,0:T(8,128)(2,1)} copy(bf16[128,2048]{1,0:T(8,128)(2,1)} %get-tuple-element.12) | data formatting | bytes 1048576
  154.3 1.6 %copy.12 = f32[1,128,384]{2,1,0:T(8,128)} copy(f32[1,128,384]{2,1,0:T(8,128)} %bitcast.5) | data formatting | bytes 393216

commit v4 on v3

--- a/solution.py
+++ b/solution.py
@@ -257,11 +257,9 @@
     for r in range(2):
         rs_copy(r, 0, r).start()
     rs_copy(0, 0, 2).start()
+    lax.fori_loop(0, 2, down_tile(1), 0)
     rs_free(2)
-    lax.fori_loop(0, 2, down_tile(1), 0)
-    rs_tied(1)
     lax.fori_loop(2, NX, down_tile(1), 0)
-    rs_free(3)
 
     def add_into(dst, *others):
         total = dst[...].astype(F32)
@@ -334,22 +332,23 @@
         if k == NY // 2:
             ring_y2.begin()
     ring_y2.forward(1, True)
+    rs_tied(1)
     for k in (2, 6, 1, 7, 0):
         add_into(a2.at[k], r2.at[k])
     core_copy(3, 0).wait_recv()
     for jj in range(2):
         add_into(a1.at[3, jj], r1.at[3, jj])
+    ring_y2.forward(1, False)
     ring_x1.forward(1, False)
     ring_y2.forward(2, True)
-    ring_y2.forward(1, False)
+    rs_free(3)
+    ring_y2.forward(2, False)
+    ring_y2.forward(3, True)
     rs_tied(2)
-    ring_y2.forward(3, True)
-    ring_y2.forward(2, False)
     ring_x1.finish()
     ring_y1.begin()
     ring_y1.forward(1, True)
     ring_y2.forward(3, False)
-    rs_tied(3)
     ring_y1.forward(2, True)
     ring_y1.forward(1, False)
     ring_y2.finish()
@@ -358,7 +357,12 @@
     ring_y1.forward(3, True)
     ring_y1.forward(2, False)
     ring_x2.forward(1, False)
+    rs_tied(3)
     ring_y1.forward(3, False)
+    ring_x2.finish()
+    dg_ref[MID:, :] = a2[0, 3].astype(F32)
+    ring_y1.finish()
+    dg_ref[:MID, :] = a1[3, 0, yh].astype(F32)
 
     mine = pl.ds(OWN, ROWS)
     for h in (1, 0):
@@ -374,11 +378,6 @@
     for k in range(ids_ref.shape[0]):
         picked = jnp.where(ids_ref[k : k + 1, :] == names, gates, 0.0)
         gg_ref[k : k + 1, :] = jnp.sum(picked, axis=0, keepdims=True)
-
-    ring_x2.finish()
-    dg_ref[MID:, :] = a2[0, 3].astype(F32)
-    ring_y1.finish()
-    dg_ref[:MID, :] = a1[3, 0, yh].astype(F32)
 
     for copy in sent + weight_first + weight_core + weight_relay:
         copy.wait_send()
@@ -393,6 +392,12 @@
             core_copy(q, half).wait_send()
     for ring in (ring_x1, ring_y1, ring_y2, ring_x2):
         ring.drain()
+
+
+def finish(tok_ref, gates_ref, down_ref, tok_out, gates_out, down_out):
+    tok_out[...] = tok_ref[...]
+    gates_out[...] = gates_ref[...].astype(BF16)
+    down_out[...] = down_ref[...]
 
 
 def shards(tokens, cotangent, expert_ids, gate_weights, w_up, w_down):
@@ -457,7 +462,18 @@
         ),
         name="expert_backward",
     )(tokens, cotangent, w_up, w_down, expert_ids.T, gate_weights.T)
-    return token_grad, gates.T.astype(BF16), down[None]
+    token_grad, gates, down = pl.pallas_call(
+        finish,
+        out_shape=(
+            jax.ShapeDtypeStruct(token_grad.shape, BF16),
+            jax.ShapeDtypeStruct(gates.shape, BF16),
+            jax.ShapeDtypeStruct(down.shape, F32),
+        ),
+        in_specs=[local] * 3,
+        out_specs=[local] * 3,
+        name="finish",
+    )(token_grad, gates, down)
+    return token_grad, gates.T, down[None]
 
 
 def solution(mesh):

time: 156 us -> 146 us (0.936)
  the two profiles are of different devices: /device:TPU:4 before, /device:TPU:1 now
where the time goes in v4:
time: 146 us; the launch traced here: 144 us
  Pallas kernels  144 us (99%)
    pallas_call x1, Pallas kernels, shards(): pl.pallas_call(kernel, out_shape=(jax.ShapeDtypeStruct((rows, width), BF1...  142 us

profile of v4, /device:TPU:1, one launch (start us, length us, event | category | flops | bytes accessed | tf_op | source)
XLA Modules:
  0.0 144.2 jit_solution(10202661719452383924)
XLA Ops:
  0.6 141.6 %expert_backward.1 = (bf16[128,2048]{1,0:T(8,128)(2,1)}, f32[8,128]{1,0:T(8,128)}, f32[128,384]{1,0:T(8,128)}) custom-call(bf16[128,2048]{1,0:T(8,128)(2,1)} %x_ref.1, bf16[128,2048]{1,0:T(8,128)(2,1)} %dy_ref.1, bf16[1,2048,384]{2,1,0:T(8,128)(2,1)} %wu_ref.1, bf16[1,2048,384]{2,1,0:T(8,128)(2,1)} %wd_ref.1, s32[8,128]{1,0:T(8,128)} %bitcast.4, ...), custom_call_target="tpu_custom_call" | custom-call | tf_op jit(solution)/shard_map/expert_backward/pallas_call | solution.py:410
  142.2 2.0 %finish.1 = (bf16[128,2048]{1,0:T(8,128)(2,1)}, bf16[8,128]{1,0:T(8,128)(2,1)}, f32[128,384]{1,0:T(8,128)}) custom-call(bf16[128,2048]{1,0:T(8,128)(2,1)} %get-tuple-element.9.tok_ref, f32[8,128]{1,0:T(8,128)} %get-tuple-element.10.gates_ref, f32[128,384]{1,0:T(8,128)} %get-tuple-element.11.down_ref), custom_call_target="tpu_custom_call" | custom-call | tf_op jit(solution)/shard_map/finish/pallas_call | solution.py:465

commit v5 on v4

--- a/solution.py
+++ b/solution.py
@@ -11,7 +11,7 @@
 NY = 2 * NYH
 ROWS = 128
 LANES = 128
-HALF = 1024
+QUART = 512
 EXP = 32
 MID = 64
 
@@ -195,12 +195,13 @@
             return carry
         return body
 
-    cols = (pl.ds(0, HALF), pl.ds(HALF, width - HALF))
+    cols = [pl.ds(c * QUART, QUART) for c in range(4)]
+    GATES = 4
     back = (zdev[1], zdev[0])
 
     def rs_copy(r, t, h):
         k = slot(4 - t, r)
-        if h == 2:
+        if h == GATES:
             src, dst = pg.at[k], rg.at[r, t]
         else:
             src, dst = pb.at[pl.ds(k * ROWS, ROWS), cols[h]], rb.at[r, t, :, cols[h]]
@@ -209,7 +210,7 @@
     def rs_add(r, t, h):
         rs_copy(r, t - 1, h).wait_recv()
         k = slot(4 - t, r)
-        if h == 2:
+        if h == GATES:
             pg[k] = (pg[k].astype(F32) + rg[r, t - 1].astype(F32)).astype(BF16)
         else:
             row = pl.ds(k * ROWS, ROWS)
@@ -218,15 +219,18 @@
         rs_copy(r, t, h).start()
 
     def rs_free(t):
-        for r in range(2):
-            rs_add(r, t, 1 - r)
-
-    def rs_tied(t):
-        for r in range(2):
-            rs_add(r, t, r)
-        for r in range(2):
-            if t > 1 or r == 0:
-                rs_add(r, t, 2)
+        for c in range(2):
+            for r in range(2):
+                rs_add(r, t, 2 * (1 - r) + c)
+
+    def rs_tied(t, parts=(0, 1)):
+        for c in parts:
+            for r in range(2):
+                rs_add(r, t, 2 * r + c)
+        if 1 in parts:
+            for r in range(2):
+                if t > 1 or r == 0:
+                    rs_add(r, t, GATES)
 
     for arr in (0, 1, 2):
         arrive(arr, 1)
@@ -248,15 +252,17 @@
     arrive(1, 3)
     arrive(2, 3)
     compute(4, 2)
-    for r in range(2):
-        rs_copy(r, 1, 1 - r).start()
-    rs_copy(1, 1, 2).start()
+    for c in range(2):
+        for r in range(2):
+            rs_copy(r, 1, 2 * (1 - r) + c).start()
+    rs_copy(1, 1, GATES).start()
     for arr in (0, 1, 2):
         arrive(arr, 4)
     compute(NZ - 1, 1)
-    for r in range(2):
-        rs_copy(r, 0, r).start()
-    rs_copy(0, 0, 2).start()
+    for c in range(2):
+        for r in range(2):
+            rs_copy(r, 0, 2 * r + c).start()
+    rs_copy(0, 0, GATES).start()
     lax.fori_loop(0, 2, down_tile(1), 0)
     rs_free(2)
     lax.fori_loop(2, NX, down_tile(1), 0)
@@ -351,13 +357,14 @@
     ring_y2.forward(3, False)
     ring_y1.forward(2, True)
     ring_y1.forward(1, False)
+    rs_tied(3, (0,))
     ring_y2.finish()
     ring_x2.begin()
     ring_x2.forward(1, True)
     ring_y1.forward(3, True)
     ring_y1.forward(2, False)
+    rs_tied(3, (1,))
     ring_x2.forward(1, False)
-    rs_tied(3)
     ring_y1.forward(3, False)
     ring_x2.finish()
     dg_ref[MID:, :] = a2[0, 3].astype(F32)
@@ -365,15 +372,14 @@
     dg_ref[:MID, :] = a1[3, 0, yh].astype(F32)
 
     mine = pl.ds(OWN, ROWS)
-    for h in (1, 0):
+    for h in (0, 2, 1, 3):
         for r in range(2):
-            rs_copy(r, 3, r ^ h).wait_recv()
-    for h in range(2):
+            rs_copy(r, 3, h).wait_recv()
         tok_ref[:, cols[h]] = (
             pb[mine, cols[h]].astype(F32) + rb[0, 3, :, cols[h]].astype(F32) + rb[1, 3, :, cols[h]].astype(F32)
         ).astype(BF16)
     for r in range(2):
-        rs_copy(r, 3, 2).wait_recv()
+        rs_copy(r, 3, GATES).wait_recv()
     gates = pg[NZ - 2].astype(F32) + rg[0, 3].astype(F32) + rg[1, 3].astype(F32)
     for k in range(ids_ref.shape[0]):
         picked = jnp.where(ids_ref[k : k + 1, :] == names, gates, 0.0)
@@ -383,8 +389,8 @@
         copy.wait_send()
     for r in range(2):
         for t in range(4):
-            for h in range(3):
-                if t == 0 and h != (r if h < 2 else 2 + r):
+            for h in range(5):
+                if t == 0 and h not in ((0, 1, GATES) if r == 0 else (2, 3)):
                     continue
                 rs_copy(r, t, h).wait_send()
     for q in range(NX):
@@ -448,8 +454,8 @@
             dma((3, 2, 5)),
             dma((2, 2, 3)),
             dma((2, 2, 3)),
-            dma((2, 4, 3)),
-            dma((2, 4, 3)),
+            dma((2, 4, 5)),
+            dma((2, 4, 5)),
             dma((NX, 2)),
             dma((NX, 2)),
             dma((2, 2, 2, 2)),

time: 146 us -> 144 us (0.986)
  no operation moved by 1% of the time
where the time goes in v5:
time: 144 us; the launch traced here: 143 us
  Pallas kernels  143 us (99%)
    pallas_call x1, Pallas kernels, shards(): pl.pallas_call(kernel, out_shape=(jax.ShapeDtypeStruct((rows, width), BF1...  141 us

profile of v5, /device:TPU:1, one launch (start us, length us, event | category | flops | bytes accessed | tf_op | source)
XLA Modules:
  0.0 143.5 jit_solution(2908619053670456923)
XLA Ops:
  0.6 140.8 %expert_backward.1 = (bf16[128,2048]{1,0:T(8,128)(2,1)}, f32[8,128]{1,0:T(8,128)}, f32[128,384]{1,0:T(8,128)}) custom-call(bf16[128,2048]{1,0:T(8,128)(2,1)} %x_ref.1, bf16[128,2048]{1,0:T(8,128)(2,1)} %dy_ref.1, bf16[1,2048,384]{2,1,0:T(8,128)(2,1)} %wu_ref.1, bf16[1,2048,384]{2,1,0:T(8,128)(2,1)} %wd_ref.1, s32[8,128]{1,0:T(8,128)} %bitcast.4, ...), custom_call_target="tpu_custom_call" | custom-call | tf_op jit(solution)/shard_map/expert_backward/pallas_call | solution.py:416
  141.5 2.0 %finish.1 = (bf16[128,2048]{1,0:T(8,128)(2,1)}, bf16[8,128]{1,0:T(8,128)(2,1)}, f32[128,384]{1,0:T(8,128)}) custom-call(bf16[128,2048]{1,0:T(8,128)(2,1)} %get-tuple-element.9.tok_ref, f32[8,128]{1,0:T(8,128)} %get-tuple-element.10.gates_ref, f32[128,384]{1,0:T(8,128)} %get-tuple-element.11.down_ref), custom_call_target="tpu_custom_call" | custom-call | tf_op jit(solution)/shard_map/finish/pallas_call | solution.py:471

commit v6 on v5

--- a/solution.py
+++ b/solution.py
@@ -118,7 +118,7 @@
     chunk = 32
     slots = [((yl if j % 2 == 0 else 1 - yl) * NZ + z) * 2 + (core if j < 2 else 1 - core) for j in range(4)]
 
-    def compute(k, blocks):
+    def compute(k, blocks, ready=None):
         base, size = k * ROWS, blocks * ROWS
         rows = pl.ds(base, size)
         for b in range(blocks):
@@ -161,7 +161,16 @@
                 gp[:size, :], wu[at, :], (((1,), (1,)), ((), ())), preferred_element_type=F32).astype(BF16)
             return carry
 
-        lax.fori_loop(0, width // 512, columns, 0)
+        if ready is None:
+            lax.fori_loop(0, width // 512, columns, 0)
+            return
+        before = None
+        for t in (0, 2, 1, 3):
+            columns(t, 0)
+            if before is not None:
+                ready(before)
+            before = t
+        ready(before)
 
     def core_copy(q, part):
         src, dst = ((s1.at[q], r1.at[q]), (s2.at[:, q], r2.at[:, q]))[part]
@@ -258,10 +267,7 @@
     rs_copy(1, 1, GATES).start()
     for arr in (0, 1, 2):
         arrive(arr, 4)
-    compute(NZ - 1, 1)
-    for c in range(2):
-        for r in range(2):
-            rs_copy(r, 0, 2 * r + c).start()
+    compute(NZ - 1, 1, lambda t: rs_copy(t // 2, 0, t).start())
     rs_copy(0, 0, GATES).start()
     lax.fori_loop(0, 2, down_tile(1), 0)
     rs_free(2)
@@ -349,8 +355,9 @@
     ring_y2.forward(2, True)
     rs_free(3)
     ring_y2.forward(2, False)
+    rs_tied(2, (0,))
     ring_y2.forward(3, True)
-    rs_tied(2)
+    rs_tied(2, (1,))
     ring_x1.finish()
     ring_y1.begin()
     ring_y1.forward(1, True)

time: 144 us -> 143 us (level)
  no operation moved by 1% of the time
where the time goes in v6:
time: 143 us
  Pallas kernels  142 us (99%)
    pallas_call x1, Pallas kernels, shards(): pl.pallas_call(kernel, out_shape=(jax.ShapeDtypeStruct((rows, width), BF1...  140 us

profile of v6, /device:TPU:1, one launch (start us, length us, event | category | flops | bytes accessed | tf_op | source)
XLA Modules:
  0.0 143.1 jit_solution(11633160658712177075)
XLA Ops:
  0.6 140.5 %expert_backward.1 = (bf16[128,2048]{1,0:T(8,128)(2,1)}, f32[8,128]{1,0:T(8,128)}, f32[128,384]{1,0:T(8,128)}) custom-call(bf16[128,2048]{1,0:T(8,128)(2,1)} %x_ref.1, bf16[128,2048]{1,0:T(8,128)(2,1)} %dy_ref.1, bf16[1,2048,384]{2,1,0:T(8,128)(2,1)} %wu_ref.1, bf16[1,2048,384]{2,1,0:T(8,128)(2,1)} %wd_ref.1, s32[8,128]{1,0:T(8,128)} %bitcast.4, ...), custom_call_target="tpu_custom_call" | custom-call | tf_op jit(solution)/shard_map/expert_backward/pallas_call | solution.py:423
  141.1 2.0 %finish.1 = (bf16[128,2048]{1,0:T(8,128)(2,1)}, bf16[8,128]{1,0:T(8,128)(2,1)}, f32[128,384]{1,0:T(8,128)}) custom-call(bf16[128,2048]{1,0:T(8,128)(2,1)} %get-tuple-element.9.tok_ref, f32[8,128]{1,0:T(8,128)} %get-tuple-element.10.gates_ref, f32[128,384]{1,0:T(8,128)} %get-tuple-element.11.down_ref), custom_call_target="tpu_custom_call" | custom-call | tf_op jit(solution)/shard_map/finish/pallas_call | solution.py:478
